TPU v7x, 32 devices: a whole 2x2x4 slice. The times are simulated.
32 devices in a mesh: leaf: 8 (over z, x), pair: 4 (over y, core).
Axes of the slice: x: 2, y: 2, z: 4, core: 2. Of those that a mesh axis runs over, the one named last changes fastest.
Arguments:
- points: float32 [64, 65536], P(None, ('pair', 'leaf')), may hold values from -6 to 6
- inv_scales: float32 [64], replicated, may hold values from 0.05 to 0.3
- direction: float32 [32, 65536], P(None, ('pair', 'leaf')), may hold values from -6 to 6
- residual: float32 [32, 65536], P(None, ('pair', 'leaf'))
- skeleton: int32 [32, 32], P(('pair', 'leaf')), may hold values from 0 to 2047, as said below
Outputs:
- product: float32 [32, 65536], P(None, ('pair', 'leaf'))
- dots: float32 [2, 32], replicated
Inputs may be any that keep to these rules, and one draw needn't show every extreme that they name: `skeleton`: each row holds 32 distinct indices of points inside its own block of 2048, among them the block's first and last point.
All inputs are finite; a program needn't handle non-finite values.
Results may differ from a plain program's by a relative error of at most 0.0003.
Values sent between devices are 32-bit elements; how exact they have to be, the bound alone decides.
A program may use at most 64 MiB of HBM per device.

v0:
```python
import math

import jax
import jax.numpy as jnp
from jax import lax
from jax.sharding import PartitionSpec as P

root_three = math.sqrt(3.0)
nugget = 0.5
far_weight = 0.125


def extended(cells, sides, width):
    for axis, dim in sides:
        count = lax.axis_size(axis)
        ends = count - 1
        head = lax.slice_in_dim(cells, 0, width, axis=dim)
        tail = lax.slice_in_dim(cells, cells.shape[dim] - width, cells.shape[dim], axis=dim)
        cells = jnp.concatenate(
            [
                lax.ppermute(tail, axis, [(i, (i + 1) % count) for i in range(ends)]),
                cells,
                lax.ppermute(head, axis, [((i + 1) % count, i) for i in range(ends)]),
            ],
            axis=dim,
        )
    return cells


def matern(left, right):
    norm_left = jnp.sum(left * left, axis=0)
    norm_right = jnp.sum(right * right, axis=0)
    cross = lax.dot_general(
        left,
        right,
        (((0,), (0,)), ((), ())),
        precision=lax.Precision.HIGHEST,
        preferred_element_type=jnp.float32,
    )
    dist_sq = norm_left[:, None] + norm_right[None, :] - 2.0 * cross
    scaled_dist = root_three * jnp.sqrt(jnp.maximum(dist_sq, 0.0))
    return (1.0 + scaled_dist) * jnp.exp(-scaled_dist)


def matmul(left, right):
    return jnp.dot(left, right, precision=lax.Precision.HIGHEST, preferred_element_type=jnp.float32)


def matmul_nt(left, right):
    return lax.dot_general(
        left,
        right,
        (((1,), (1,)), ((), ())),
        precision=lax.Precision.HIGHEST,
        preferred_element_type=jnp.float32,
    )


def on_device(points, inv_scales, direction, residual, skeleton):
    feats = points.shape[0]
    block_pts = points.shape[1]
    rhs = direction.shape[0]
    skel_count = skeleton.shape[1]
    row_blk = 128
    nsteps = block_pts // row_blk
    starts = jnp.arange(nsteps, dtype=jnp.int32) * row_blk
    nleaf = lax.axis_size("leaf")
    npair = lax.axis_size("pair")
    leaf_pos = lax.axis_index("leaf")
    pair_pos = lax.axis_index("pair")
    scaled = points * inv_scales[:, None]
    packed = jnp.concatenate([scaled, direction], axis=0)
    wide = extended(packed, (("leaf", 1),), block_pts)
    cols_z = wide[:feats]
    cols_v = wide[feats:]

    def row_part(start):
        z_rows = lax.dynamic_slice_in_dim(scaled, start, row_blk, 1)
        return matmul(cols_v, matern(cols_z, z_rows))

    parts = lax.map(row_part, starts)
    near = jnp.transpose(parts, (1, 0, 2)).reshape(rhs, block_pts)
    own_skel = jnp.take(scaled, skeleton[0], axis=1)
    spread = matern(scaled, own_skel)
    coeff = matmul(direction, spread)
    skel_pack = jnp.concatenate([own_skel, coeff], axis=0)
    subtree = lax.all_gather(skel_pack, "leaf", axis=1, tiled=True)
    piece = lax.all_gather(subtree, "pair", axis=1, tiled=True)
    count = piece.shape[1]
    column = jnp.arange(count, dtype=jnp.int32)
    block_id = column // skel_count
    far_mask = (block_id // nleaf != pair_pos) | (jnp.abs(block_id % nleaf - leaf_pos) > 1)
    kernel = matern(piece[:feats], own_skel)
    weights = jnp.where(far_mask[:, None], kernel, 0.0)
    q_coeff = matmul(piece[feats:], weights)
    far = matmul_nt(q_coeff, spread)
    amplitude = 1.0 / math.sqrt(3.0 * block_pts)
    product = nugget * direction + amplitude * (near + far_weight * far)
    squares_local = jnp.sum(residual * residual, axis=1)
    curvature_local = jnp.sum(direction * product, axis=1)
    squares, curvature = lax.psum((squares_local, curvature_local), ("leaf", "pair"))
    total = block_pts * nleaf * npair
    dots = jnp.stack([squares, curvature], axis=0) / total
    return (product, dots)


def solution(mesh):
    return jax.shard_map(
        on_device,
        mesh=mesh,
        in_specs=(
            P(None, ("pair", "leaf")),
            P(),
            P(None, ("pair", "leaf")),
            P(None, ("pair", "leaf")),
            P(("pair", "leaf"), None),
        ),
        out_specs=(P(None, ("pair", "leaf")), P()),
        check_vma=False,
    )
```

profile of v0, /device:TPU:0, one launch (start us, length us, event | category | flops | bytes accessed | tf_op | source)
XLA Modules:
  0.0 319.7 jit_solution(5436503925950408070)
XLA Ops:
  7.2 6.4 %collective-permute-start = (f32[96,2048]{1,0:T(8,128)}, f32[96,2048]{1,0:T(8,128)}, u32[]{:S(2)}, u32[]{:S(2)}) collective-permute-start(f32[96,2048]{1,0:T(8,128)} %copy.15), channel_id=1, source_target_pairs={{0,4},{4,8},{8,12},{12,16},{16,20},{20,24},{24,28},{1,5},{5,9},{9,... | collective-permute-start | bytes 2359304 | tf_op jit(solution)/shard_map/ppermute | solution.py:21
  18.4 51.6 %all_gather.6 = f32[96,256]{0,1:T(8,128)S(1)} all-gather(f32[96,32]{0,1:T(8,128)S(1)} %pad_maximum_fusion.2), channel_id=1, replica_groups=mesh['leaf'=8,'pair'=4] {'leaf'}, dimensions={1}, use_global_device_ids=true | all-gather | bytes 110592 | tf_op jit(solution)/shard_map/all_gather | solution.py:87
  70.0 7.4 %all_gather.7 = f32[96,1024]{0,1:T(8,128)S(1)} all-gather(f32[96,256]{0,1:T(8,128)S(1)} %all_gather.6), channel_id=1, replica_groups=mesh['leaf'=8,'pair'=4] {'pair'}, dimensions={1}, use_global_device_ids=true | all-gather | bytes 491520 | tf_op jit(solution)/shard_map/all_gather | solution.py:88
  94.7 186.2 %while.12 = (s32[]{:T(128)}, f32[16,32,128]{2,1,0:T(8,128)S(1)}, f32[6144]{0:T(1024)S(1)}, s32[16]{0:T(128)S(1)}, f32[64,2048]{1,0:T(8,128)}, /*index=5*/f32[64,...) while((s32[]{:T(128)}, f32[16,32,128]{2,1,0:T(8,128)S(1)}, ...), condition=%wide.region_3.4_spmd, body=%wide.region_1.3_spmd.sunk | while | flops 912277376 | bytes 8758439 | solution.py:81
  98.4 4.7 %fusion.84 = f32[6144,128]{0,1:T(8,128)S(1)} fusion(f32[64,6144]{1,0:T(8,128)S(1)} %get-tuple-element.186, f32[128]{0:T(128)S(1)} %multiply_reduce_fusion.8, f32[6144]{0:T(1024)S(1)} %get-tuple-element.183, f32[64,2048]{1,0:T(8,128)} %get-tuple-element.185, s32[]{:T(128)S(6)} %select_n.114), kind=kOutput, calls=%fused_computation.6.clone.1 | convolution fusion | flops 607911936 | bytes 4776452 | tf_op jit(solution)/shard_map/while/body/eval_jaxpr/dot_general | solution.py:33
  103.1 3.2 %fusion.85 = f32[16,32,128]{2,1,0:T(8,128)S(1)} fusion(f32[16,32,128]{2,1,0:T(8,128)S(1)} %get-tuple-element.172, s32[]{:T(128)S(6)} %copy.28, f32[32,6144]{1,0:T(8,128)S(1)} %get-tuple-element.187, f32[6144,128]{0,1:T(8,128)S(1)} %fusion.84), kind=kOutput, calls=%fused_computation.14.clone.1 | convolution fusion | flops 304349184 | bytes 3948548 | tf_op jit(solution)/shard_map/while/body/eval_jaxpr/dot_general | solution.py:46
  110.1 4.7 %fusion.84 = f32[6144,128]{0,1:T(8,128)S(1)} fusion(f32[64,6144]{1,0:T(8,128)S(1)} %get-tuple-element.186, f32[128]{0:T(128)S(1)} %multiply_reduce_fusion.8, f32[6144]{0:T(1024)S(1)} %get-tuple-element.183, f32[64,2048]{1,0:T(8,128)} %get-tuple-element.185, s32[]{:T(128)S(6)} %select_n.114), kind=kOutput, calls=%fused_computation.6.clone.1 | convolution fusion | flops 607911936 | bytes 4776452 | tf_op jit(solution)/shard_map/while/body/eval_jaxpr/dot_general | solution.py:33
  114.8 3.2 %fusion.85 = f32[16,32,128]{2,1,0:T(8,128)S(1)} fusion(f32[16,32,128]{2,1,0:T(8,128)S(1)} %get-tuple-element.172, s32[]{:T(128)S(6)} %copy.28, f32[32,6144]{1,0:T(8,128)S(1)} %get-tuple-element.187, f32[6144,128]{0,1:T(8,128)S(1)} %fusion.84), kind=kOutput, calls=%fused_computation.14.clone.1 | convolution fusion | flops 304349184 | bytes 3948548 | tf_op jit(solution)/shard_map/while/body/eval_jaxpr/dot_general | solution.py:46
  121.7 4.7 %fusion.84 = f32[6144,128]{0,1:T(8,128)S(1)} fusion(f32[64,6144]{1,0:T(8,128)S(1)} %get-tuple-element.186, f32[128]{0:T(128)S(1)} %multiply_reduce_fusion.8, f32[6144]{0:T(1024)S(1)} %get-tuple-element.183, f32[64,2048]{1,0:T(8,128)} %get-tuple-element.185, s32[]{:T(128)S(6)} %select_n.114), kind=kOutput, calls=%fused_computation.6.clone.1 | convolution fusion | flops 607911936 | bytes 4776452 | tf_op jit(solution)/shard_map/while/body/eval_jaxpr/dot_general | solution.py:33
  126.4 3.2 %fusion.85 = f32[16,32,128]{2,1,0:T(8,128)S(1)} fusion(f32[16,32,128]{2,1,0:T(8,128)S(1)} %get-tuple-element.172, s32[]{:T(128)S(6)} %copy.28, f32[32,6144]{1,0:T(8,128)S(1)} %get-tuple-element.187, f32[6144,128]{0,1:T(8,128)S(1)} %fusion.84), kind=kOutput, calls=%fused_computation.14.clone.1 | convolution fusion | flops 304349184 | bytes 3948548 | tf_op jit(solution)/shard_map/while/body/eval_jaxpr/dot_general | solution.py:46
  133.4 4.7 %fusion.84 = f32[6144,128]{0,1:T(8,128)S(1)} fusion(f32[64,6144]{1,0:T(8,128)S(1)} %get-tuple-element.186, f32[128]{0:T(128)S(1)} %multiply_reduce_fusion.8, f32[6144]{0:T(1024)S(1)} %get-tuple-element.183, f32[64,2048]{1,0:T(8,128)} %get-tuple-element.185, s32[]{:T(128)S(6)} %select_n.114), kind=kOutput, calls=%fused_computation.6.clone.1 | convolution fusion | flops 607911936 | bytes 4776452 | tf_op jit(solution)/shard_map/while/body/eval_jaxpr/dot_general | solution.py:33
  138.1 3.2 %fusion.85 = f32[16,32,128]{2,1,0:T(8,128)S(1)} fusion(f32[16,32,128]{2,1,0:T(8,128)S(1)} %get-tuple-element.172, s32[]{:T(128)S(6)} %copy.28, f32[32,6144]{1,0:T(8,128)S(1)} %get-tuple-element.187, f32[6144,128]{0,1:T(8,128)S(1)} %fusion.84), kind=kOutput, calls=%fused_computation.14.clone.1 | convolution fusion | flops 304349184 | bytes 3948548 | tf_op jit(solution)/shard_map/while/body/eval_jaxpr/dot_general | solution.py:46
  145.0 4.7 %fusion.84 = f32[6144,128]{0,1:T(8,128)S(1)} fusion(f32[64,6144]{1,0:T(8,128)S(1)} %get-tuple-element.186, f32[128]{0:T(128)S(1)} %multiply_reduce_fusion.8, f32[6144]{0:T(1024)S(1)} %get-tuple-element.183, f32[64,2048]{1,0:T(8,128)} %get-tuple-element.185, s32[]{:T(128)S(6)} %select_n.114), kind=kOutput, calls=%fused_computation.6.clone.1 | convolution fusion | flops 607911936 | bytes 4776452 | tf_op jit(solution)/shard_map/while/body/eval_jaxpr/dot_general | solution.py:33
  149.7 3.2 %fusion.85 = f32[16,32,128]{2,1,0:T(8,128)S(1)} fusion(f32[16,32,128]{2,1,0:T(8,128)S(1)} %get-tuple-element.172, s32[]{:T(128)S(6)} %copy.28, f32[32,6144]{1,0:T(8,128)S(1)} %get-tuple-element.187, f32[6144,128]{0,1:T(8,128)S(1)} %fusion.84), kind=kOutput, calls=%fused_computation.14.clone.1 | convolution fusion | flops 304349184 | bytes 3948548 | tf_op jit(solution)/shard_map/while/body/eval_jaxpr/dot_general | solution.py:46
  156.7 4.7 %fusion.84 = f32[6144,128]{0,1:T(8,128)S(1)} fusion(f32[64,6144]{1,0:T(8,128)S(1)} %get-tuple-element.186, f32[128]{0:T(128)S(1)} %multiply_reduce_fusion.8, f32[6144]{0:T(1024)S(1)} %get-tuple-element.183, f32[64,2048]{1,0:T(8,128)} %get-tuple-element.185, s32[]{:T(128)S(6)} %select_n.114), kind=kOutput, calls=%fused_computation.6.clone.1 | convolution fusion | flops 607911936 | bytes 4776452 | tf_op jit(solution)/shard_map/while/body/eval_jaxpr/dot_general | solution.py:33
  161.4 3.2 %fusion.85 = f32[16,32,128]{2,1,0:T(8,128)S(1)} fusion(f32[16,32,128]{2,1,0:T(8,128)S(1)} %get-tuple-element.172, s32[]{:T(128)S(6)} %copy.28, f32[32,6144]{1,0:T(8,128)S(1)} %get-tuple-element.187, f32[6144,128]{0,1:T(8,128)S(1)} %fusion.84), kind=kOutput, calls=%fused_computation.14.clone.1 | convolution fusion | flops 304349184 | bytes 3948548 | tf_op jit(solution)/shard_map/while/body/eval_jaxpr/dot_general | solution.py:46
  168.3 4.7 %fusion.84 = f32[6144,128]{0,1:T(8,128)S(1)} fusion(f32[64,6144]{1,0:T(8,128)S(1)} %get-tuple-element.186, f32[128]{0:T(128)S(1)} %multiply_reduce_fusion.8, f32[6144]{0:T(1024)S(1)} %get-tuple-element.183, f32[64,2048]{1,0:T(8,128)} %get-tuple-element.185, s32[]{:T(128)S(6)} %select_n.114), kind=kOutput, calls=%fused_computation.6.clone.1 | convolution fusion | flops 607911936 | bytes 4776452 | tf_op jit(solution)/shard_map/while/body/eval_jaxpr/dot_general | solution.py:33
  180.0 4.7 %fusion.84 = f32[6144,128]{0,1:T(8,128)S(1)} fusion(f32[64,6144]{1,0:T(8,128)S(1)} %get-tuple-element.186, f32[128]{0:T(128)S(1)} %multiply_reduce_fusion.8, f32[6144]{0:T(1024)S(1)} %get-tuple-element.183, f32[64,2048]{1,0:T(8,128)} %get-tuple-element.185, s32[]{:T(128)S(6)} %select_n.114), kind=kOutput, calls=%fused_computation.6.clone.1 | convolution fusion | flops 607911936 | bytes 4776452 | tf_op jit(solution)/shard_map/while/body/eval_jaxpr/dot_general | solution.py:33
  184.7 3.2 %fusion.85 = f32[16,32,128]{2,1,0:T(8,128)S(1)} fusion(f32[16,32,128]{2,1,0:T(8,128)S(1)} %get-tuple-element.172, s32[]{:T(128)S(6)} %copy.28, f32[32,6144]{1,0:T(8,128)S(1)} %get-tuple-element.187, f32[6144,128]{0,1:T(8,128)S(1)} %fusion.84), kind=kOutput, calls=%fused_computation.14.clone.1 | convolution fusion | flops 304349184 | bytes 3948548 | tf_op jit(solution)/shard_map/while/body/eval_jaxpr/dot_general | solution.py:46
  191.6 4.7 %fusion.84 = f32[6144,128]{0,1:T(8,128)S(1)} fusion(f32[64,6144]{1,0:T(8,128)S(1)} %get-tuple-element.186, f32[128]{0:T(128)S(1)} %multiply_reduce_fusion.8, f32[6144]{0:T(1024)S(1)} %get-tuple-element.183, f32[64,2048]{1,0:T(8,128)} %get-tuple-element.185, s32[]{:T(128)S(6)} %select_n.114), kind=kOutput, calls=%fused_computation.6.clone.1 | convolution fusion | flops 607911936 | bytes 4776452 | tf_op jit(solution)/shard_map/while/body/eval_jaxpr/dot_general | solution.py:33
  196.3 3.2 %fusion.85 = f32[16,32,128]{2,1,0:T(8,128)S(1)} fusion(f32[16,32,128]{2,1,0:T(8,128)S(1)} %get-tuple-element.172, s32[]{:T(128)S(6)} %copy.28, f32[32,6144]{1,0:T(8,128)S(1)} %get-tuple-element.187, f32[6144,128]{0,1:T(8,128)S(1)} %fusion.84), kind=kOutput, calls=%fused_computation.14.clone.1 | convolution fusion | flops 304349184 | bytes 3948548 | tf_op jit(solution)/shard_map/while/body/eval_jaxpr/dot_general | solution.py:46
  203.3 4.7 %fusion.84 = f32[6144,128]{0,1:T(8,128)S(1)} fusion(f32[64,6144]{1,0:T(8,128)S(1)} %get-tuple-element.186, f32[128]{0:T(128)S(1)} %multiply_reduce_fusion.8, f32[6144]{0:T(1024)S(1)} %get-tuple-element.183, f32[64,2048]{1,0:T(8,128)} %get-tuple-element.185, s32[]{:T(128)S(6)} %select_n.114), kind=kOutput, calls=%fused_computation.6.clone.1 | convolution fusion | flops 607911936 | bytes 4776452 | tf_op jit(solution)/shard_map/while/body/eval_jaxpr/dot_general | solution.py:33
  214.9 4.7 %fusion.84 = f32[6144,128]{0,1:T(8,128)S(1)} fusion(f32[64,6144]{1,0:T(8,128)S(1)} %get-tuple-element.186, f32[128]{0:T(128)S(1)} %multiply_reduce_fusion.8, f32[6144]{0:T(1024)S(1)} %get-tuple-element.183, f32[64,2048]{1,0:T(8,128)} %get-tuple-element.185, s32[]{:T(128)S(6)} %select_n.114), kind=kOutput, calls=%fused_computation.6.clone.1 | convolution fusion | flops 607911936 | bytes 4776452 | tf_op jit(solution)/shard_map/while/body/eval_jaxpr/dot_general | solution.py:33
  226.5 4.7 %fusion.84 = f32[6144,128]{0,1:T(8,128)S(1)} fusion(f32[64,6144]{1,0:T(8,128)S(1)} %get-tuple-element.186, f32[128]{0:T(128)S(1)} %multiply_reduce_fusion.8, f32[6144]{0:T(1024)S(1)} %get-tuple-element.183, f32[64,2048]{1,0:T(8,128)} %get-tuple-element.185, s32[]{:T(128)S(6)} %select_n.114), kind=kOutput, calls=%fused_computation.6.clone.1 | convolution fusion | flops 607911936 | bytes 4776452 | tf_op jit(solution)/shard_map/while/body/eval_jaxpr/dot_general | solution.py:33
  238.2 4.7 %fusion.84 = f32[6144,128]{0,1:T(8,128)S(1)} fusion(f32[64,6144]{1,0:T(8,128)S(1)} %get-tuple-element.186, f32[128]{0:T(128)S(1)} %multiply_reduce_fusion.8, f32[6144]{0:T(1024)S(1)} %get-tuple-element.183, f32[64,2048]{1,0:T(8,128)} %get-tuple-element.185, s32[]{:T(128)S(6)} %select_n.114), kind=kOutput, calls=%fused_computation.6.clone.1 | convolution fusion | flops 607911936 | bytes 4776452 | tf_op jit(solution)/shard_map/while/body/eval_jaxpr/dot_general | solution.py:33
  242.9 3.2 %fusion.85 = f32[16,32,128]{2,1,0:T(8,128)S(1)} fusion(f32[16,32,128]{2,1,0:T(8,128)S(1)} %get-tuple-element.172, s32[]{:T(128)S(6)} %copy.28, f32[32,6144]{1,0:T(8,128)S(1)} %get-tuple-element.187, f32[6144,128]{0,1:T(8,128)S(1)} %fusion.84), kind=kOutput, calls=%fused_computation.14.clone.1 | convolution fusion | flops 304349184 | bytes 3948548 | tf_op jit(solution)/shard_map/while/body/eval_jaxpr/dot_general | solution.py:46
  249.8 4.7 %fusion.84 = f32[6144,128]{0,1:T(8,128)S(1)} fusion(f32[64,6144]{1,0:T(8,128)S(1)} %get-tuple-element.186, f32[128]{0:T(128)S(1)} %multiply_reduce_fusion.8, f32[6144]{0:T(1024)S(1)} %get-tuple-element.183, f32[64,2048]{1,0:T(8,128)} %get-tuple-element.185, s32[]{:T(128)S(6)} %select_n.114), kind=kOutput, calls=%fused_computation.6.clone.1 | convolution fusion | flops 607911936 | bytes 4776452 | tf_op jit(solution)/shard_map/while/body/eval_jaxpr/dot_general | solution.py:33
  254.6 3.2 %fusion.85 = f32[16,32,128]{2,1,0:T(8,128)S(1)} fusion(f32[16,32,128]{2,1,0:T(8,128)S(1)} %get-tuple-element.172, s32[]{:T(128)S(6)} %copy.28, f32[32,6144]{1,0:T(8,128)S(1)} %get-tuple-element.187, f32[6144,128]{0,1:T(8,128)S(1)} %fusion.84), kind=kOutput, calls=%fused_computation.14.clone.1 | convolution fusion | flops 304349184 | bytes 3948548 | tf_op jit(solution)/shard_map/while/body/eval_jaxpr/dot_general | solution.py:46
  261.5 4.7 %fusion.84 = f32[6144,128]{0,1:T(8,128)S(1)} fusion(f32[64,6144]{1,0:T(8,128)S(1)} %get-tuple-element.186, f32[128]{0:T(128)S(1)} %multiply_reduce_fusion.8, f32[6144]{0:T(1024)S(1)} %get-tuple-element.183, f32[64,2048]{1,0:T(8,128)} %get-tuple-element.185, s32[]{:T(128)S(6)} %select_n.114), kind=kOutput, calls=%fused_computation.6.clone.1 | convolution fusion | flops 607911936 | bytes 4776452 | tf_op jit(solution)/shard_map/while/body/eval_jaxpr/dot_general | solution.py:33
  273.0 4.6 %fusion.84 = f32[6144,128]{0,1:T(8,128)S(1)} fusion(f32[64,6144]{1,0:T(8,128)S(1)} %get-tuple-element.186, f32[128]{0:T(128)S(1)} %multiply_reduce_fusion.8, f32[6144]{0:T(1024)S(1)} %get-tuple-element.183, f32[64,2048]{1,0:T(8,128)} %get-tuple-element.185, s32[]{:T(128)S(6)} %select_n.114), kind=kOutput, calls=%fused_computation.6.clone.1 | convolution fusion | flops 607911936 | bytes 4776452 | tf_op jit(solution)/shard_map/while/body/eval_jaxpr/dot_general | solution.py:33
  277.7 3.2 %fusion.85 = f32[16,32,128]{2,1,0:T(8,128)S(1)} fusion(f32[16,32,128]{2,1,0:T(8,128)S(1)} %get-tuple-element.172, s32[]{:T(128)S(6)} %copy.28, f32[32,6144]{1,0:T(8,128)S(1)} %get-tuple-element.187, f32[6144,128]{0,1:T(8,128)S(1)} %fusion.84), kind=kOutput, calls=%fused_computation.14.clone.1 | convolution fusion | flops 304349184 | bytes 3948548 | tf_op jit(solution)/shard_map/while/body/eval_jaxpr/dot_general | solution.py:46
  282.2 36.9 %all-reduce = (f32[1,32]{1,0:T(1,128)S(1)}, f32[1,32]{1,0:T(1,128)S(1)}) all-reduce(f32[1,32]{1,0:T(1,128)S(1)} %bitcast.54, f32[1,32]{1,0:T(1,128)S(1)} %bitcast.53), channel_id=1, replica_groups=mesh['leaf'=8,'pair'=4] {'leaf','pair'}, use_global_device_ids=true, to_apply=%region_10.11 | all-reduce | flops 64 | bytes 512 | tf_op jit(solution)/shard_map/psum | solution.py:101
  (80 shorter events, 72.0 us)
Async XLA Ops:
  3.3 10.3 %copy-start.4 = (s32[1,32]{1,0:T(1,128)S(1)}, s32[1,32]{1,0:T(1,128)}, u32[]{:S(2)}) copy-start(s32[1,32]{1,0:T(1,128)} %param.11) | copy-start | bytes 388
  4.7 13.3 %copy-start = (f32[32,2048]{1,0:T(8,128)S(1)}, f32[32,2048]{1,0:T(8,128)}, u32[]{:S(2)}) copy-start(f32[32,2048]{1,0:T(8,128)} %param.9) | copy-start | bytes 786436
  5.9 73.5 %collective-permute-start.1 = (f32[96,2048]{1,0:T(8,128)}, f32[96,2048]{1,0:T(8,128)}, u32[]{:S(2)}, u32[]{:S(2)}) collective-permute-start(f32[96,2048]{1,0:T(8,128)} %copy.15), channel_id=1, source_target_pairs={{4,0},{8,4},{12,8},{16,12},{20,16},{24,20},{28,24},{5,1},{9,5},{13... | collective-permute-start | bytes 2359304 | tf_op jit(solution)/shard_map/ppermute | solution.py:23
  7.2 73.7 %collective-permute-start = (f32[96,2048]{1,0:T(8,128)}, f32[96,2048]{1,0:T(8,128)}, u32[]{:S(2)}, u32[]{:S(2)}) collective-permute-start(f32[96,2048]{1,0:T(8,128)} %copy.15), channel_id=1, source_target_pairs={{0,4},{4,8},{8,12},{12,16},{16,20},{20,24},{24,28},{1,5},{5,9},{9,... | collective-permute-start | bytes 2359304 | tf_op jit(solution)/shard_map/ppermute | solution.py:21
  17.9 61.4 %copy-start.1 = (f32[2048,32]{0,1:T(8,128)}, f32[2048,32]{0,1:T(8,128)S(1)}, u32[]{:S(2)}) copy-start(f32[2048,32]{0,1:T(8,128)S(1)} %exponential_multiply_fusion) | copy-start | bytes 786436
  92.3 2.4 copy-start.3
  94.7 186.2 %copy-start.2 = (f32[2048,32]{0,1:T(8,128)S(1)}, f32[2048,32]{0,1:T(8,128)}, u32[]{:S(2)}) copy-start(f32[2048,32]{0,1:T(8,128)} %copy-done.1) | copy-start | bytes 786436
where the time goes:
time: 323 us; the launch traced here: 320 us
  matrix products  132 us (41%)
  blocking collectives  95.9 us (30%)
  loops' own time  33.7 us (10%)
  local copies, waits for them, and re-layouts  27.5 us (9%)
  other arithmetic  22.5 us (7%)
  starting transfers between devices  7.71 us (2%)
    dot_general x18, matrix products, matern(): lax.dot_general(left, right, (((0,), (0,)), ((), ())), precision=lax.Prec...  77.2 us
    dot_general x18, matrix products, matmul(): jnp.dot(left, right, precision=lax.Precision.HIGHEST, preferred_element_t...  53.1 us
    all_gather x1, blocking collectives, on_device(): subtree = lax.all_gather(skel_pack, 'leaf', axis=1, tiled=True)  51.6 us
    psum x1, blocking collectives, on_device(): lax.psum((squares_local, curvature_local), ('leaf', 'pair'))  36.9 us
    another operation x1, loops' own time, on_device(): parts = lax.map(row_part, starts)  33.7 us
    reduce_sum x17, other arithmetic, matern(): norm_right = jnp.sum(right * right, axis=0)  15.1 us
    dynamic_slice x16, local copies, waits for them, and re-layouts, on_device(): parts = lax.map(row_part, starts)  10.7 us
    all_gather x1, blocking collectives, on_device(): piece = lax.all_gather(subtree, 'pair', axis=1, tiled=True)  7.37 us
  transfers between devices with their start and end apart: 2, of which 0 were waited for; matrix products, arithmetic and copies ran while one was open for 3% of the time, Pallas kernels for 0%

commit v1 on v0

v1 whole, which is shorter than its diff:
```python
import functools
import math

import jax
import jax.numpy as jnp
from jax import lax
from jax.experimental import pallas as pl
from jax.experimental.pallas import tpu as pltpu
from jax.sharding import PartitionSpec as P

root_three = math.sqrt(3.0)
neg_log2e = -1.4426950408889634
nugget = 0.5
far_weight = 0.125
tiny = 1e-30
f32 = jnp.float32
bf16 = jnp.bfloat16
HI = lax.Precision.HIGHEST
TI = 256
TJ = 256
CH = 256


def matern_of(u):
    u = jnp.maximum(u, tiny)
    t = u * lax.rsqrt(u)
    return (1.0 + t) * jnp.exp2(t * neg_log2e)


def dot_nn(a, b):
    return lax.dot_general(a, b, (((1,), (0,)), ((), ())), precision=HI, preferred_element_type=f32)


def dot_nt(a, b):
    return lax.dot_general(a, b, (((1,), (1,)), ((), ())), precision=HI, preferred_element_type=f32)


def dot_tn(a, b):
    return lax.dot_general(a, b, (((0,), (0,)), ((), ())), precision=HI, preferred_element_type=f32)


def bdot(a, b):
    return jnp.dot(a, b, preferred_element_type=f32)


def split(x):
    h = x.astype(bf16)
    return h, (x - h.astype(f32)).astype(bf16)


def kernel(
    nleaf, npair, nblk_total,
    pts_ref, inv_ref, dir_ref, res_ref, skel_ref,
    prod_ref, dots_ref,
    halo_p, halo_d, b_ref, nb_ref, st_ref, ns_ref, dd_ref, acc_ref, ks_ref, ag_ref, red_a, red_b, tmp_ref,
    hs_sem, hr_sem, as_sem, ar_sem, bs_sem, br_sem, cs_sem, cr_sem, ds_sem, dr_sem,
):
    feats, n = pts_ref.shape
    rhs = dir_ref.shape[0]
    nskel = skel_ref.shape[1]
    leaf = lax.axis_index("leaf")
    pair = lax.axis_index("pair")

    def remote(src, dst, ss, rs, **dev):
        return pltpu.make_async_remote_copy(
            src_ref=src, dst_ref=dst, send_sem=ss, recv_sem=rs, device_id=dev,
            device_id_type=pl.DeviceIdType.MESH)

    def leaf_peer(k):
        return lax.rem(leaf + k, nleaf)

    def pair_peer(k):
        return lax.rem(pair + k, npair)

    barrier = pltpu.get_barrier_semaphore()
    for k in range(1, nleaf):
        pl.semaphore_signal(barrier, inc=1, device_id={"leaf": leaf_peer(k)}, device_id_type=pl.DeviceIdType.MESH)
    for k in range(1, npair):
        pl.semaphore_signal(barrier, inc=1, device_id={"pair": pair_peer(k)}, device_id_type=pl.DeviceIdType.MESH)
    pl.semaphore_wait(barrier, nleaf - 1 + npair - 1)

    has_left = leaf > 0
    has_right = leaf < nleaf - 1
    to_right = [
        remote(pts_ref, halo_p.at[0], hs_sem.at[0], hr_sem.at[0], leaf=leaf_peer(1)),
        remote(dir_ref, halo_d.at[0], hs_sem.at[1], hr_sem.at[1], leaf=leaf_peer(1)),
    ]
    to_left = [
        remote(pts_ref, halo_p.at[1], hs_sem.at[2], hr_sem.at[2], leaf=leaf_peer(nleaf - 1)),
        remote(dir_ref, halo_d.at[1], hs_sem.at[3], hr_sem.at[3], leaf=leaf_peer(nleaf - 1)),
    ]

    @pl.when(has_right)
    def _():
        for c in to_right:
            c.start()

    @pl.when(has_left)
    def _():
        for c in to_left:
            c.start()

    eye = lax.broadcasted_iota(jnp.int32, (feats, feats), 0) == lax.broadcasted_iota(jnp.int32, (feats, feats), 1)
    inv_col = jnp.sum(jnp.where(eye, jnp.broadcast_to(inv_ref[...], (feats, feats)), 0.0), axis=1, keepdims=True) * root_three

    def prep(p_src, d_src, own):
        @pl.loop(0, n // CH)
        def _(ci):
            cols = pl.ds(pl.multiple_of(ci * CH, CH), CH)
            p = p_src[:, cols] * inv_col
            h, l = split(p)
            hf, lf = h.astype(f32), l.astype(f32)
            q = hf + lf
            norm = jnp.sum(q * q, axis=0, keepdims=True)
            if own:
                b_ref[:, cols] = jnp.concatenate([h, l, h, l], axis=0)
                nb_ref[:, cols] = jnp.broadcast_to(norm, (8, CH))
            h2, l2 = hf * -2.0, lf * -2.0
            stack = jnp.concatenate([h2, h2, l2, l2], axis=0)
            st_ref[cols, :] = stack.T.astype(bf16)
            ns_ref[cols, :] = jnp.broadcast_to(norm, (128, CH)).T
            dh, dl = split(d_src[:, cols])
            dd_ref[:, cols] = jnp.concatenate([dh, dl], axis=0)

    def near_block(first):
        @pl.loop(0, n // TJ)
        def _(jt):
            cols = pl.ds(pl.multiple_of(jt * TJ, TJ), TJ)
            b = b_ref[:, cols]
            nb = nb_ref[0:1, cols]
            if first:
                a1 = jnp.zeros((2 * rhs, TJ), f32)
                a2 = jnp.zeros((rhs, TJ), f32)
            else:
                a1 = acc_ref[: 2 * rhs, cols]
                a2 = acc_ref[2 * rhs :, cols]
            for it in range(n // TI):
                rows = slice(it * TI, (it + 1) * TI)
                cross = bdot(st_ref[rows, :], b)
                nsr = ns_ref[rows, :]
                u = cross + jnp.concatenate([nsr] * (TJ // 128), axis=1) + nb
                k = matern_of(u)
                kh, kl = split(k)
                a1 = a1 + bdot(dd_ref[:, rows], kh)
                a2 = a2 + bdot(dd_ref[:rhs, rows], kl)
            acc_ref[: 2 * rhs, cols] = a1
            acc_ref[2 * rhs :, cols] = a2

    prep(pts_ref, dir_ref, True)

    onehot = (lax.broadcasted_iota(jnp.int32, (n, nskel), 0) == jnp.broadcast_to(skel_ref[...], (n, nskel)))
    onehot = jnp.where(onehot, 1.0, 0.0).astype(bf16)
    p_all = pts_ref[...] * inv_col
    s0 = p_all.astype(bf16)
    r1 = p_all - s0.astype(f32)
    s1 = r1.astype(bf16)
    s2 = (r1 - s1.astype(f32)).astype(bf16)
    skel_pts = bdot(s0, onehot) + bdot(s1, onehot) + bdot(s2, onehot)
    skel_rows = skel_pts.T
    norm_s = jnp.sum(skel_rows * skel_rows, axis=1, keepdims=True)
    norm_p = jnp.sum(p_all * p_all, axis=0, keepdims=True)
    ks = matern_of(norm_s + norm_p - 2.0 * dot_nn(skel_rows, p_all))
    ks_ref[...] = ks
    coeff_t = dot_nt(ks, dir_ref[...])
    pad = jnp.zeros((nskel, 128 - feats - rhs), f32)
    pack = jnp.concatenate([skel_rows, coeff_t, pad], axis=1)
    my_rows = pl.ds(pl.multiple_of(leaf * nskel, 8), nskel)
    ag_ref[pair, my_rows, :] = pack
    tmp_ref[...] = jnp.concatenate([skel_rows, jnp.zeros((nskel, 128 - feats), f32)], axis=1)

    stage_a = [
        remote(ag_ref.at[pair, my_rows, :], ag_ref.at[pair, my_rows, :], as_sem.at[k], ar_sem.at[k], leaf=leaf_peer(k))
        for k in range(1, nleaf)
    ]
    for c in stage_a:
        c.start()

    near_block(True)

    for k, c in enumerate(stage_a, 1):
        src_rows = pl.ds(pl.multiple_of(lax.rem(leaf + nleaf - k, nleaf) * nskel, 8), nskel)
        remote(ag_ref.at[pair, src_rows, :], ag_ref.at[pair, src_rows, :], as_sem.at[k], ar_sem.at[k], leaf=leaf_peer(k)).wait_recv()
    for c in stage_a:
        c.wait_send()
    stage_b = [
        remote(ag_ref.at[pair], ag_ref.at[pair], bs_sem.at[k], br_sem.at[k], pair=pair_peer(k))
        for k in range(1, npair)
    ]
    for c in stage_b:
        c.start()

    @pl.when(has_left)
    def _():
        for c in to_right:
            c.wait_recv()
        prep(halo_p.at[0], halo_d.at[0], False)
        near_block(False)

    for k, c in enumerate(stage_b, 1):
        src = lax.rem(pair + npair - k, npair)
        remote(ag_ref.at[src], ag_ref.at[src], bs_sem.at[k], br_sem.at[k], pair=pair_peer(k)).wait_recv()
    for c in stage_b:
        c.wait_send()

    width = nleaf * nskel
    own_rows = tmp_ref[...]
    own_norm = jnp.sum(own_rows * own_rows, axis=1, keepdims=True)
    is_pt = jnp.where(lax.broadcasted_iota(jnp.int32, (8, 128), 1) < feats, 1.0, 0.0)
    column_leaf = lax.div(lax.broadcasted_iota(jnp.int32, (nskel, width), 1), nskel)
    near_mask = jnp.abs(column_leaf - leaf) <= 1
    q_t = jnp.zeros((nskel, 128), f32)
    for p in range(npair):
        all_rows = ag_ref[p]
        cross = dot_nt(own_rows, all_rows)
        norm_all = dot_nt(is_pt, all_rows * all_rows)[0:1, :]
        w = matern_of(own_norm + norm_all - 2.0 * cross)
        same = jnp.full((nskel, width), pair, jnp.int32) == p
        w = jnp.where(jnp.logical_and(same, near_mask), 0.0, w)
        q_t = q_t + dot_nn(w, all_rows)
    q_t = q_t[:, feats : feats + rhs]
    prod_ref[...] = dot_tn(q_t, ks_ref[...])

    @pl.when(has_right)
    def _():
        for c in to_left:
            c.wait_recv()
        prep(halo_p.at[1], halo_d.at[1], False)
        near_block(False)

    amplitude = 1.0 / math.sqrt(3.0 * n)
    near = acc_ref[:rhs, :] + acc_ref[rhs : 2 * rhs, :] + acc_ref[2 * rhs :, :]
    direction = dir_ref[...]
    product = nugget * direction + amplitude * (near + far_weight * prod_ref[...])
    prod_ref[...] = product
    residual = res_ref[...]
    squares = jnp.sum(residual * residual, axis=1, keepdims=True)
    curvature = jnp.sum(direction * product, axis=1, keepdims=True)
    lane = lax.broadcasted_iota(jnp.int32, (rhs, 128), 1)
    both = jnp.where(lane == 0, squares, jnp.where(lane == 1, curvature, 0.0))
    both = jnp.concatenate([both, jnp.zeros((128 - rhs, 128), f32)], axis=0).T[0:8, :]
    red_a[leaf] = both
    sends = [
        remote(red_a.at[leaf], red_a.at[leaf], cs_sem.at[k], cr_sem.at[k], leaf=leaf_peer(k))
        for k in range(1, nleaf)
    ]
    for c in sends:
        c.start()
    for k in range(1, nleaf):
        src = lax.rem(leaf + nleaf - k, nleaf)
        remote(red_a.at[src], red_a.at[src], cs_sem.at[k], cr_sem.at[k], leaf=leaf_peer(k)).wait_recv()
    total = red_a[0]
    for k in range(1, nleaf):
        total = total + red_a[k]
    red_b[pair] = total
    sends_b = [
        remote(red_b.at[pair], red_b.at[pair], ds_sem.at[k], dr_sem.at[k], pair=pair_peer(k))
        for k in range(1, npair)
    ]
    for c in sends_b:
        c.start()
    for k in range(1, npair):
        src = lax.rem(pair + npair - k, npair)
        remote(red_b.at[src], red_b.at[src], ds_sem.at[k], dr_sem.at[k], pair=pair_peer(k)).wait_recv()
    total = red_b[0]
    for k in range(1, npair):
        total = total + red_b[k]
    dots_ref[...] = total[0:2, :rhs] * (1.0 / nblk_total)
    for c in sends + sends_b:
        c.wait_send()

    @pl.when(has_right)
    def _():
        for c in to_right:
            c.wait_send()

    @pl.when(has_left)
    def _():
        for c in to_left:
            c.wait_send()


def on_device(points, inv_scales, direction, residual, skeleton):
    feats, n = points.shape
    rhs = direction.shape[0]
    nskel = skeleton.shape[1]
    nleaf = lax.axis_size("leaf")
    npair = lax.axis_size("pair")
    vmem = pl.BlockSpec(memory_space=pltpu.VMEM)
    dma = pltpu.SemaphoreType.DMA
    return pl.pallas_call(
        functools.partial(kernel, nleaf, npair, n * nleaf * npair),
        out_shape=(jax.ShapeDtypeStruct((rhs, n), f32), jax.ShapeDtypeStruct((2, rhs), f32)),
        in_specs=[vmem] * 5,
        out_specs=(vmem, vmem),
        scratch_shapes=[
            pltpu.VMEM((2, feats, n), f32),
            pltpu.VMEM((2, rhs, n), f32),
            pltpu.VMEM((4 * feats, n), bf16),
            pltpu.VMEM((8, n), f32),
            pltpu.VMEM((n, 4 * feats), bf16),
            pltpu.VMEM((n, 128), f32),
            pltpu.VMEM((2 * rhs, n), bf16),
            pltpu.VMEM((3 * rhs, n), f32),
            pltpu.VMEM((nskel, n), f32),
            pltpu.VMEM((npair, nleaf * nskel, 128), f32),
            pltpu.VMEM((nleaf, 8, 128), f32),
            pltpu.VMEM((npair, 8, 128), f32),
            pltpu.VMEM((nskel, 128), f32),
            dma((4,)), dma((4,)),
            dma((nleaf,)), dma((nleaf,)),
            dma((npair,)), dma((npair,)),
            dma((nleaf,)), dma((nleaf,)),
            dma((npair,)), dma((npair,)),
        ],
        compiler_params=pltpu.CompilerParams(collective_id=0, has_side_effects=True, vmem_limit_bytes=60 * 1024 * 1024),
        name="matern_step",
    )(points, inv_scales.reshape(1, feats), direction, residual, skeleton)


def solution(mesh):
    return jax.shard_map(
        on_device,
        mesh=mesh,
        in_specs=(
            P(None, ("pair", "leaf")),
            P(),
            P(None, ("pair", "leaf")),
            P(None, ("pair", "leaf")),
            P(("pair", "leaf"), None),
        ),
        out_specs=(P(None, ("pair", "leaf")), P()),
        check_vma=False,
    )
```

time: 323 us -> 78.5 us (0.24)
  matrix products: 132 us -> 0 us
  blocking collectives: 95.9 us -> 0 us
  Pallas kernels: 0 us -> 75.5 us
  loops' own time: 33.7 us -> 0 us
  local copies, waits for them, and re-layouts: 27.5 us -> 2.24 us
  other arithmetic: 22.5 us -> 0 us
  starting transfers between devices: 7.71 us -> 0 us
    dot_general x37 -> x0, matrix products: 132 us -> none  [the longest x18 77.2 us: matern(): lax.dot_general(left, right, (((0,), (0,)), ((), ())), precision=lax.Prec...]
    pallas_call x0 -> x1, Pallas kernels: none -> 75.5 us  [on_device(): pl.pallas_call(functools.partial(kernel, nleaf, npair, n * nleaf * npair)...]
    all_gather x2 -> x0, blocking collectives: 58.9 us -> none  [the longest x1 51.6 us: on_device(): subtree = lax.all_gather(skel_pack, 'leaf', axis=1, tiled=True)]
    psum x1 -> x0, blocking collectives: 36.9 us -> none  [on_device(): lax.psum((squares_local, curvature_local), ('leaf', 'pair'))]
    another operation x1 -> x0, loops' own time: 33.7 us -> none  [on_device(): parts = lax.map(row_part, starts)]
    reduce_sum x20 -> x0, other arithmetic: 17.4 us -> none  [the longest x17 15.1 us: matern(): norm_right = jnp.sum(right * right, axis=0)]
    dynamic_slice x16 -> x0, local copies, waits for them, and re-layouts: 10.7 us -> none  [on_device(): parts = lax.map(row_part, starts)]
    ppermute x2 -> x0, starting transfers between devices: 7.71 us -> none  [the longest x1 6.43 us: extended(): lax.ppermute(tail, axis, [(i, (i + 1) % count) for i in range(ends)])]
  transfers between devices with their start and end apart: 2 -> 0, of which waited for: 0 -> 0; matrix products, arithmetic and copies ran while one was open for 3% -> 0% of each run, Pallas kernels for 0% -> 0%
where the time goes in v1:
time: 78.5 us; the launch traced here: 78.3 us
  Pallas kernels  75.5 us (96%)
  local copies, waits for them, and re-layouts  2.24 us (3%)
    pallas_call x1, Pallas kernels, on_device(): pl.pallas_call(functools.partial(kernel, nleaf, npair, n * nleaf * npair)...  75.5 us
    unnamed x4, local copies, waits for them, and re-layouts  2.24 us

profile of v1, /device:TPU:0, one launch (start us, length us, event | category | flops | bytes accessed | tf_op | source)
XLA Modules:
  0.0 78.3 jit_solution(6566303468635428606)
XLA Ops:
  0.6 75.5 %matern_step.1 = (f32[32,2048]{1,0:T(8,128)}, f32[2,32]{1,0:T(2,128)}) custom-call(f32[64,2048]{1,0:T(8,128)} %pts_ref.1, f32[1,64]{1,0:T(1,128)} %bitcast.1, f32[32,2048]{1,0:T(8,128)} %dir_ref.1, f32[32,2048]{1,0:T(8,128)} %res_ref.1, s32[1,32]{1,0:T(1,128)} %skel_ref.1), custom_call_target="tpu_custom_call" | custom-call | tf_op jit(solution)/shard_map/matern_step/pallas_call | solution.py:290
  76.1 0.0 copy-start
  76.1 1.7 %copy.9 = f32[32,2048]{1,0:T(8,128)} copy(f32[32,2048]{1,0:T(8,128)} %get-tuple-element.4) | data formatting | bytes 524288
  77.8 0.0 copy-done
  77.8 0.6 copy.10
Async XLA Ops:
  76.1 1.7 %copy-start = (f32[2,32]{1,0:T(2,128)S(1)}, f32[2,32]{1,0:T(2,128)}, u32[]{:S(2)}) copy-start(f32[2,32]{1,0:T(2,128)} %get-tuple-element.5) | copy-start | bytes 772

commit v2 on v1

--- a/solution.py
+++ b/solution.py
@@ -17,7 +17,8 @@
 bf16 = jnp.bfloat16
 HI = lax.Precision.HIGHEST
 TI = 256
-TJ = 256
+CC = 512
+FIRST = 2
 CH = 256
 
 
@@ -43,6 +44,10 @@
     return jnp.dot(a, b, preferred_element_type=f32)
 
 
+def bdot_nt(a, b):
+    return lax.dot_general(a, b, (((1,), (1,)), ((), ())), preferred_element_type=f32)
+
+
 def split(x):
     h = x.astype(bf16)
     return h, (x - h.astype(f32)).astype(bf16)
@@ -52,8 +57,8 @@
     nleaf, npair, nblk_total,
     pts_ref, inv_ref, dir_ref, res_ref, skel_ref,
     prod_ref, dots_ref,
-    halo_p, halo_d, b_ref, nb_ref, st_ref, ns_ref, dd_ref, acc_ref, ks_ref, ag_ref, red_a, red_b, tmp_ref,
-    hs_sem, hr_sem, as_sem, ar_sem, bs_sem, br_sem, cs_sem, cr_sem, ds_sem, dr_sem,
+    halo_p, halo_d, ret_out, ret_in, b_ref, nb_ref, st_ref, ns_ref, dd_ref, acc_ref, ks_ref, ag_ref, red_a, red_b, tmp_ref,
+    hs_sem, hr_sem, es_sem, er_sem, as_sem, ar_sem, bs_sem, br_sem, cs_sem, cr_sem, ds_sem, dr_sem,
 ):
     feats, n = pts_ref.shape
     rhs = dir_ref.shape[0]
@@ -81,72 +86,112 @@
 
     has_left = leaf > 0
     has_right = leaf < nleaf - 1
-    to_right = [
-        remote(pts_ref, halo_p.at[0], hs_sem.at[0], hr_sem.at[0], leaf=leaf_peer(1)),
-        remote(dir_ref, halo_d.at[0], hs_sem.at[1], hr_sem.at[1], leaf=leaf_peer(1)),
-    ]
-    to_left = [
-        remote(pts_ref, halo_p.at[1], hs_sem.at[2], hr_sem.at[2], leaf=leaf_peer(nleaf - 1)),
-        remote(dir_ref, halo_d.at[1], hs_sem.at[3], hr_sem.at[3], leaf=leaf_peer(nleaf - 1)),
-    ]
-
-    @pl.when(has_right)
-    def _():
-        for c in to_right:
-            c.start()
-
-    @pl.when(has_left)
-    def _():
-        for c in to_left:
-            c.start()
+    left = leaf_peer(nleaf - 1)
+    right = leaf_peer(1)
+
+    def chunk(ci):
+        return pl.ds(pl.multiple_of(ci * CC, CC), CC)
+
+    def halo(ci):
+        cols = chunk(ci)
+        return (
+            remote(pts_ref.at[:, cols], halo_p.at[:, cols], hs_sem.at[0, ci], hr_sem.at[0, ci], leaf=left),
+            remote(dir_ref.at[:, cols], halo_d.at[:, cols], hs_sem.at[1, ci], hr_sem.at[1, ci], leaf=left),
+        )
+
+    def give_back(ci):
+        cols = chunk(ci)
+        return remote(ret_out.at[:, cols], ret_in.at[:, cols], es_sem.at[ci], er_sem.at[ci], leaf=right)
+
+    def send_halo(lo, hi):
+        @pl.when(has_left)
+        def _():
+            for ci in range(lo, hi):
+                for c in halo(ci):
+                    c.start()
+
+    send_halo(0, FIRST)
 
     eye = lax.broadcasted_iota(jnp.int32, (feats, feats), 0) == lax.broadcasted_iota(jnp.int32, (feats, feats), 1)
     inv_col = jnp.sum(jnp.where(eye, jnp.broadcast_to(inv_ref[...], (feats, feats)), 0.0), axis=1, keepdims=True) * root_three
 
-    def prep(p_src, d_src, own):
-        @pl.loop(0, n // CH)
-        def _(ci):
-            cols = pl.ds(pl.multiple_of(ci * CH, CH), CH)
-            p = p_src[:, cols] * inv_col
-            h, l = split(p)
-            hf, lf = h.astype(f32), l.astype(f32)
-            q = hf + lf
-            norm = jnp.sum(q * q, axis=0, keepdims=True)
-            if own:
-                b_ref[:, cols] = jnp.concatenate([h, l, h, l], axis=0)
-                nb_ref[:, cols] = jnp.broadcast_to(norm, (8, CH))
-            h2, l2 = hf * -2.0, lf * -2.0
-            stack = jnp.concatenate([h2, h2, l2, l2], axis=0)
-            st_ref[cols, :] = stack.T.astype(bf16)
-            ns_ref[cols, :] = jnp.broadcast_to(norm, (128, CH)).T
-            dh, dl = split(d_src[:, cols])
-            dd_ref[:, cols] = jnp.concatenate([dh, dl], axis=0)
-
-    def near_block(first):
-        @pl.loop(0, n // TJ)
+    def halves(p_src, d_src, cols):
+        p = p_src[:, cols] * inv_col
+        h, l = split(p)
+        hf, lf = h.astype(f32), l.astype(f32)
+        q = hf + lf
+        norm = jnp.sum(q * q, axis=0, keepdims=True)
+        dh, dl = split(d_src[:, cols])
+        return jnp.concatenate([h, l, h, l], axis=0), jnp.concatenate([dh, dl], axis=0), hf, lf, norm
+
+    @pl.loop(0, n // CH)
+    def _(ci):
+        cols = pl.ds(pl.multiple_of(ci * CH, CH), CH)
+        b, dd, hf, lf, norm = halves(pts_ref, dir_ref, cols)
+        b_ref[:, cols] = b
+        dd_ref[:, cols] = dd
+        nb_ref[:, cols] = jnp.broadcast_to(norm, (8, CH))
+        h2, l2 = hf * -2.0, lf * -2.0
+        st_ref[cols, :] = jnp.concatenate([h2, h2, l2, l2], axis=0).T.astype(bf16)
+        ns_ref[cols, :] = jnp.broadcast_to(norm, (128, CH)).T
+        acc_ref[:, cols] = jnp.zeros((rhs, CH), f32)
+
+    nt = n // TI
+
+    def tiles(rows_of, count, b, nb):
+        nxt = bdot(st_ref[rows_of(0), :], b)
+        for i in range(count):
+            cross = nxt
+            if i + 1 < count:
+                nxt = bdot(st_ref[rows_of(i + 1), :], b)
+            u = cross + jnp.concatenate([ns_ref[rows_of(i), :]] * (b.shape[1] // 128), axis=1) + nb
+            kh, kl = split(matern_of(u))
+            yield i, kh, kl
+
+    def own_block():
+        @pl.loop(0, nt)
         def _(jt):
-            cols = pl.ds(pl.multiple_of(jt * TJ, TJ), TJ)
+            cols = pl.ds(pl.multiple_of(jt * TI, TI), TI)
             b = b_ref[:, cols]
             nb = nb_ref[0:1, cols]
-            if first:
-                a1 = jnp.zeros((2 * rhs, TJ), f32)
-                a2 = jnp.zeros((rhs, TJ), f32)
-            else:
-                a1 = acc_ref[: 2 * rhs, cols]
-                a2 = acc_ref[2 * rhs :, cols]
-            for it in range(n // TI):
-                rows = slice(it * TI, (it + 1) * TI)
-                cross = bdot(st_ref[rows, :], b)
-                nsr = ns_ref[rows, :]
-                u = cross + jnp.concatenate([nsr] * (TJ // 128), axis=1) + nb
-                k = matern_of(u)
-                kh, kl = split(k)
+            ddj = dd_ref[:, cols]
+            a1 = jnp.zeros((2 * rhs, TI), f32)
+            a2 = jnp.zeros((rhs, TI), f32)
+
+            def rows_of(d):
+                return pl.ds(pl.multiple_of(lax.rem(jt + nt - d, nt) * TI, TI), TI)
+
+            later = []
+            for d, kh, kl in tiles(rows_of, nt // 2 + 1, b, nb):
+                rows = rows_of(d)
                 a1 = a1 + bdot(dd_ref[:, rows], kh)
                 a2 = a2 + bdot(dd_ref[:rhs, rows], kl)
-            acc_ref[: 2 * rhs, cols] = a1
-            acc_ref[2 * rhs :, cols] = a2
-
-    prep(pts_ref, dir_ref, True)
+                if 0 < d and 2 * d < nt:
+                    r1 = bdot_nt(ddj, kh)
+                    later.append((rows, r1[:rhs] + r1[rhs:] + bdot_nt(ddj[:rhs], kl)))
+            acc_ref[:, cols] += a1[:rhs] + a1[rhs:] + a2
+            for rows, part in later:
+                acc_ref[:, rows] += part
+
+    def pair_chunk(ci):
+        for c in halo(ci):
+            c.wait_recv()
+
+        @pl.loop(0, CC // TI)
+        def _(half):
+            cols = pl.ds(pl.multiple_of(ci * CC + half * TI, TI), TI)
+            b, ddj, _, _, nb = halves(halo_p, halo_d, cols)
+            a1 = jnp.zeros((2 * rhs, TI), f32)
+            a2 = jnp.zeros((rhs, TI), f32)
+            for it, kh, kl in tiles(lambda i: slice(i * TI, (i + 1) * TI), nt, b, nb):
+                rows = slice(it * TI, (it + 1) * TI)
+                a1 = a1 + bdot(dd_ref[:, rows], kh)
+                a2 = a2 + bdot(dd_ref[:rhs, rows], kl)
+                r1 = bdot_nt(ddj, kh)
+                acc_ref[:, rows] += r1[:rhs] + r1[rhs:] + bdot_nt(ddj[:rhs], kl)
+            ret_out[:, cols] = a1[:rhs] + a1[rhs:] + a2
+
+        give_back(ci).start()
 
     onehot = (lax.broadcasted_iota(jnp.int32, (n, nskel), 0) == jnp.broadcast_to(skel_ref[...], (n, nskel)))
     onehot = jnp.where(onehot, 1.0, 0.0).astype(bf16)
@@ -175,26 +220,29 @@
     for c in stage_a:
         c.start()
 
-    near_block(True)
-
-    for k, c in enumerate(stage_a, 1):
-        src_rows = pl.ds(pl.multiple_of(lax.rem(leaf + nleaf - k, nleaf) * nskel, 8), nskel)
-        remote(ag_ref.at[pair, src_rows, :], ag_ref.at[pair, src_rows, :], as_sem.at[k], ar_sem.at[k], leaf=leaf_peer(k)).wait_recv()
-    for c in stage_a:
-        c.wait_send()
+    send_halo(FIRST, n // CC)
+    own_block()
+
     stage_b = [
         remote(ag_ref.at[pair], ag_ref.at[pair], bs_sem.at[k], br_sem.at[k], pair=pair_peer(k))
         for k in range(1, npair)
     ]
-    for c in stage_b:
-        c.start()
-
-    @pl.when(has_left)
-    def _():
-        for c in to_right:
-            c.wait_recv()
-        prep(halo_p.at[0], halo_d.at[0], False)
-        near_block(False)
+
+    @pl.loop(0, n // CC)
+    def _(ci):
+        @pl.when(ci == n // CC - 1)
+        def _():
+            for k, c in enumerate(stage_a, 1):
+                src_rows = pl.ds(pl.multiple_of(lax.rem(leaf + nleaf - k, nleaf) * nskel, 8), nskel)
+                remote(ag_ref.at[pair, src_rows, :], ag_ref.at[pair, src_rows, :], as_sem.at[k], ar_sem.at[k], leaf=leaf_peer(k)).wait_recv()
+            for c in stage_a:
+                c.wait_send()
+            for c in stage_b:
+                c.start()
+
+        @pl.when(has_right)
+        def _():
+            pair_chunk(ci)
 
     for k, c in enumerate(stage_b, 1):
         src = lax.rem(pair + npair - k, npair)
@@ -218,19 +266,18 @@
         w = jnp.where(jnp.logical_and(same, near_mask), 0.0, w)
         q_t = q_t + dot_nn(w, all_rows)
     q_t = q_t[:, feats : feats + rhs]
-    prod_ref[...] = dot_tn(q_t, ks_ref[...])
-
-    @pl.when(has_right)
+    far = dot_tn(q_t, ks_ref[...])
+    prod_ref[...] = far_weight * far + acc_ref[...]
+
+    @pl.when(has_left)
     def _():
-        for c in to_left:
-            c.wait_recv()
-        prep(halo_p.at[1], halo_d.at[1], False)
-        near_block(False)
+        for ci in range(n // CC):
+            give_back(ci).wait_recv()
+        prod_ref[...] += ret_in[...]
 
     amplitude = 1.0 / math.sqrt(3.0 * n)
-    near = acc_ref[:rhs, :] + acc_ref[rhs : 2 * rhs, :] + acc_ref[2 * rhs :, :]
     direction = dir_ref[...]
-    product = nugget * direction + amplitude * (near + far_weight * prod_ref[...])
+    product = nugget * direction + amplitude * prod_ref[...]
     prod_ref[...] = product
     residual = res_ref[...]
     squares = jnp.sum(residual * residual, axis=1, keepdims=True)
@@ -270,13 +317,14 @@
 
     @pl.when(has_right)
     def _():
-        for c in to_right:
-            c.wait_send()
+        for ci in range(n // CC):
+            give_back(ci).wait_send()
 
     @pl.when(has_left)
     def _():
-        for c in to_left:
-            c.wait_send()
+        for ci in range(n // CC):
+            for c in halo(ci):
+                c.wait_send()
 
 
 def on_device(points, inv_scales, direction, residual, skeleton):
@@ -293,20 +341,23 @@
         in_specs=[vmem] * 5,
         out_specs=(vmem, vmem),
         scratch_shapes=[
-            pltpu.VMEM((2, feats, n), f32),
-            pltpu.VMEM((2, rhs, n), f32),
+            pltpu.VMEM((feats, n), f32),
+            pltpu.VMEM((rhs, n), f32),
+            pltpu.VMEM((rhs, n), f32),
+            pltpu.VMEM((rhs, n), f32),
             pltpu.VMEM((4 * feats, n), bf16),
             pltpu.VMEM((8, n), f32),
             pltpu.VMEM((n, 4 * feats), bf16),
             pltpu.VMEM((n, 128), f32),
             pltpu.VMEM((2 * rhs, n), bf16),
-            pltpu.VMEM((3 * rhs, n), f32),
+            pltpu.VMEM((rhs, n), f32),
             pltpu.VMEM((nskel, n), f32),
             pltpu.VMEM((npair, nleaf * nskel, 128), f32),
             pltpu.VMEM((nleaf, 8, 128), f32),
             pltpu.VMEM((npair, 8, 128), f32),
             pltpu.VMEM((nskel, 128), f32),
-            dma((4,)), dma((4,)),
+            dma((2, n // CC)), dma((2, n // CC)),
+            dma((n // CC,)), dma((n // CC,)),
             dma((nleaf,)), dma((nleaf,)),
             dma((npair,)), dma((npair,)),
             dma((nleaf,)), dma((nleaf,)),

time: 78.5 us -> 55.4 us (0.71)
  Pallas kernels: 75.5 us -> 52.3 us
    pallas_call x1, Pallas kernels: 75.5 us -> 52.3 us  [on_device(): pl.pallas_call(functools.partial(kernel, nleaf, npair, n * nleaf * npair)...]
where the time goes in v2:
time: 55.4 us; the launch traced here: 55.2 us
  Pallas kernels  52.3 us (94%)
  local copies, waits for them, and re-layouts  2.24 us (4%)
  between operations  0.65 us (1%)
    pallas_call x1, Pallas kernels, on_device(): pl.pallas_call(functools.partial(kernel, nleaf, npair, n * nleaf * npair)...  52.3 us
    unnamed x4, local copies, waits for them, and re-layouts  2.24 us

profile of v2, /device:TPU:0, one launch (start us, length us, event | category | flops | bytes accessed | tf_op | source)
XLA Modules:
  0.0 55.2 jit_solution(16701341995840464145)
XLA Ops:
  0.6 52.3 %matern_step.1 = (f32[32,2048]{1,0:T(8,128)}, f32[2,32]{1,0:T(2,128)}) custom-call(f32[64,2048]{1,0:T(8,128)} %pts_ref.1, f32[1,64]{1,0:T(1,128)} %bitcast.1, f32[32,2048]{1,0:T(8,128)} %dir_ref.1, f32[32,2048]{1,0:T(8,128)} %res_ref.1, s32[1,32]{1,0:T(1,128)} %skel_ref.1), custom_call_target="tpu_custom_call" | custom-call | tf_op jit(solution)/shard_map/matern_step/pallas_call | solution.py:338
  53.0 0.0 copy-start
  53.0 1.7 %copy.9 = f32[32,2048]{1,0:T(8,128)} copy(f32[32,2048]{1,0:T(8,128)} %get-tuple-element.4) | data formatting | bytes 524288
  54.6 0.0 copy-done
  54.6 0.6 %copy.10 = f32[2,32]{1,0:T(2,128)} copy(f32[2,32]{1,0:T(2,128)S(1)} %copy-done) | data formatting | bytes 512
Async XLA Ops:
  53.0 1.7 %copy-start = (f32[2,32]{1,0:T(2,128)S(1)}, f32[2,32]{1,0:T(2,128)}, u32[]{:S(2)}) copy-start(f32[2,32]{1,0:T(2,128)} %get-tuple-element.5) | copy-start | bytes 772

commit v3 on v2

--- a/solution.py
+++ b/solution.py
@@ -15,7 +15,6 @@
 tiny = 1e-30
 f32 = jnp.float32
 bf16 = jnp.bfloat16
-HI = lax.Precision.HIGHEST
 TI = 256
 CC = 512
 FIRST = 2
@@ -28,18 +27,6 @@
     return (1.0 + t) * jnp.exp2(t * neg_log2e)
 
 
-def dot_nn(a, b):
-    return lax.dot_general(a, b, (((1,), (0,)), ((), ())), precision=HI, preferred_element_type=f32)
-
-
-def dot_nt(a, b):
-    return lax.dot_general(a, b, (((1,), (1,)), ((), ())), precision=HI, preferred_element_type=f32)
-
-
-def dot_tn(a, b):
-    return lax.dot_general(a, b, (((0,), (0,)), ((), ())), precision=HI, preferred_element_type=f32)
-
-
 def bdot(a, b):
     return jnp.dot(a, b, preferred_element_type=f32)
 
@@ -57,7 +44,7 @@
     nleaf, npair, nblk_total,
     pts_ref, inv_ref, dir_ref, res_ref, skel_ref,
     prod_ref, dots_ref,
-    halo_p, halo_d, ret_out, ret_in, b_ref, nb_ref, st_ref, ns_ref, dd_ref, acc_ref, ks_ref, ag_ref, red_a, red_b, tmp_ref,
+    halo_p, halo_d, ret_out, ret_in, b_ref, nb_ref, st_ref, ns_ref, dd_ref, acc_ref, pacc_ref, ks_ref, ag_ref, red_a, red_b, tmp_ref,
     hs_sem, hr_sem, es_sem, er_sem, as_sem, ar_sem, bs_sem, br_sem, cs_sem, cr_sem, ds_sem, dr_sem,
 ):
     feats, n = pts_ref.shape
@@ -135,6 +122,7 @@
         st_ref[cols, :] = jnp.concatenate([h2, h2, l2, l2], axis=0).T.astype(bf16)
         ns_ref[cols, :] = jnp.broadcast_to(norm, (128, CH)).T
         acc_ref[:, cols] = jnp.zeros((rhs, CH), f32)
+        pacc_ref[:, cols] = jnp.zeros((rhs, CH), f32)
 
     nt = n // TI
 
@@ -145,8 +133,11 @@
             if i + 1 < count:
                 nxt = bdot(st_ref[rows_of(i + 1), :], b)
             u = cross + jnp.concatenate([ns_ref[rows_of(i), :]] * (b.shape[1] // 128), axis=1) + nb
-            kh, kl = split(matern_of(u))
-            yield i, kh, kl
+            now = (i,) + split(matern_of(u))
+            if i:
+                yield held
+            held = now
+        yield held
 
     def own_block():
         @pl.loop(0, nt)
@@ -188,25 +179,23 @@
                 a1 = a1 + bdot(dd_ref[:, rows], kh)
                 a2 = a2 + bdot(dd_ref[:rhs, rows], kl)
                 r1 = bdot_nt(ddj, kh)
-                acc_ref[:, rows] += r1[:rhs] + r1[rhs:] + bdot_nt(ddj[:rhs], kl)
+                pacc_ref[:, rows] += r1[:rhs] + r1[rhs:] + bdot_nt(ddj[:rhs], kl)
             ret_out[:, cols] = a1[:rhs] + a1[rhs:] + a2
 
         give_back(ci).start()
 
     onehot = (lax.broadcasted_iota(jnp.int32, (n, nskel), 0) == jnp.broadcast_to(skel_ref[...], (n, nskel)))
     onehot = jnp.where(onehot, 1.0, 0.0).astype(bf16)
-    p_all = pts_ref[...] * inv_col
-    s0 = p_all.astype(bf16)
-    r1 = p_all - s0.astype(f32)
-    s1 = r1.astype(bf16)
-    s2 = (r1 - s1.astype(f32)).astype(bf16)
-    skel_pts = bdot(s0, onehot) + bdot(s1, onehot) + bdot(s2, onehot)
-    skel_rows = skel_pts.T
+    picked = bdot(b_ref[: 2 * feats, :], onehot)
+    skel_rows = (picked[:feats] + picked[feats:]).T
     norm_s = jnp.sum(skel_rows * skel_rows, axis=1, keepdims=True)
-    norm_p = jnp.sum(p_all * p_all, axis=0, keepdims=True)
-    ks = matern_of(norm_s + norm_p - 2.0 * dot_nn(skel_rows, p_all))
-    ks_ref[...] = ks
-    coeff_t = dot_nt(ks, dir_ref[...])
+    sh, sl = split(skel_rows)
+    sh, sl = sh.astype(f32) * -2.0, sl.astype(f32) * -2.0
+    cross_s = bdot(jnp.concatenate([sh, sh, sl, sl], axis=1).astype(bf16), b_ref[...])
+    ksh, ksl = split(matern_of(norm_s + nb_ref[0:1, :] + cross_s))
+    ks_ref[...] = jnp.concatenate([ksh, ksl], axis=0)
+    part = bdot_nt(ks_ref[...], dd_ref[...])
+    coeff_t = part[:nskel, :rhs] + part[:nskel, rhs:] + part[nskel:, :rhs] + part[nskel:, rhs:]
     pad = jnp.zeros((nskel, 128 - feats - rhs), f32)
     pack = jnp.concatenate([skel_rows, coeff_t, pad], axis=1)
     my_rows = pl.ds(pl.multiple_of(leaf * nskel, 8), nskel)
@@ -253,35 +242,37 @@
     width = nleaf * nskel
     own_rows = tmp_ref[...]
     own_norm = jnp.sum(own_rows * own_rows, axis=1, keepdims=True)
-    is_pt = jnp.where(lax.broadcasted_iota(jnp.int32, (8, 128), 1) < feats, 1.0, 0.0)
+    own_both = jnp.concatenate(split(own_rows), axis=0)
+    is_pt = jnp.where(lax.broadcasted_iota(jnp.int32, (8, 128), 1) < feats, 1.0, 0.0).astype(bf16)
     column_leaf = lax.div(lax.broadcasted_iota(jnp.int32, (nskel, width), 1), nskel)
     near_mask = jnp.abs(column_leaf - leaf) <= 1
     q_t = jnp.zeros((nskel, 128), f32)
     for p in range(npair):
-        all_rows = ag_ref[p]
-        cross = dot_nt(own_rows, all_rows)
-        norm_all = dot_nt(is_pt, all_rows * all_rows)[0:1, :]
-        w = matern_of(own_norm + norm_all - 2.0 * cross)
+        ah, al = split(ag_ref[p])
+        ar = ah.astype(f32) + al.astype(f32)
+        sq = ar * ar
+        s0, r1 = sq.astype(bf16), sq - sq.astype(bf16).astype(f32)
+        s1, s2 = split(r1)
+        norm_all = (bdot_nt(is_pt, s0) + bdot_nt(is_pt, s1) + bdot_nt(is_pt, s2))[0:1, :]
+        cross = bdot_nt(own_both, ah) + bdot_nt(own_both, al)
+        w = matern_of(own_norm + norm_all - 2.0 * (cross[:nskel] + cross[nskel:]))
         same = jnp.full((nskel, width), pair, jnp.int32) == p
         w = jnp.where(jnp.logical_and(same, near_mask), 0.0, w)
-        q_t = q_t + dot_nn(w, all_rows)
+        wh, wl = split(w)
+        part = bdot(jnp.concatenate([wh, wl], axis=0), ah)
+        q_t = q_t + part[:nskel] + part[nskel:] + bdot(wh, al)
     q_t = q_t[:, feats : feats + rhs]
-    far = dot_tn(q_t, ks_ref[...])
-    prod_ref[...] = far_weight * far + acc_ref[...]
-
-    @pl.when(has_left)
-    def _():
-        for ci in range(n // CC):
-            give_back(ci).wait_recv()
-        prod_ref[...] += ret_in[...]
-
+    qh, ql = split(q_t.T)
+    far = bdot(jnp.concatenate([qh, ql], axis=0), ks_ref[:nskel, :])
+    far = far[:rhs] + far[rhs:] + bdot(qh, ks_ref[nskel:, :])
     amplitude = 1.0 / math.sqrt(3.0 * n)
     direction = dir_ref[...]
-    product = nugget * direction + amplitude * prod_ref[...]
+    pair_part = amplitude * pacc_ref[...]
+    product = nugget * direction + amplitude * (acc_ref[...] + far_weight * far) + pair_part
     prod_ref[...] = product
     residual = res_ref[...]
     squares = jnp.sum(residual * residual, axis=1, keepdims=True)
-    curvature = jnp.sum(direction * product, axis=1, keepdims=True)
+    curvature = jnp.sum(direction * (product + pair_part), axis=1, keepdims=True)
     lane = lax.broadcasted_iota(jnp.int32, (rhs, 128), 1)
     both = jnp.where(lane == 0, squares, jnp.where(lane == 1, curvature, 0.0))
     both = jnp.concatenate([both, jnp.zeros((128 - rhs, 128), f32)], axis=0).T[0:8, :]
@@ -311,6 +302,13 @@
     total = red_b[0]
     for k in range(1, npair):
         total = total + red_b[k]
+
+    @pl.when(has_left)
+    def _():
+        for ci in range(n // CC):
+            give_back(ci).wait_recv()
+        prod_ref[...] += amplitude * ret_in[...]
+
     dots_ref[...] = total[0:2, :rhs] * (1.0 / nblk_total)
     for c in sends + sends_b:
         c.wait_send()
@@ -351,7 +349,8 @@
             pltpu.VMEM((n, 128), f32),
             pltpu.VMEM((2 * rhs, n), bf16),
             pltpu.VMEM((rhs, n), f32),
-            pltpu.VMEM((nskel, n), f32),
+            pltpu.VMEM((rhs, n), f32),
+            pltpu.VMEM((2 * nskel, n), bf16),
             pltpu.VMEM((npair, nleaf * nskel, 128), f32),
             pltpu.VMEM((nleaf, 8, 128), f32),
             pltpu.VMEM((npair, 8, 128), f32),

time: 55.4 us -> 45.2 us (0.82)
  Pallas kernels: 52.3 us -> 42.2 us
    pallas_call x1, Pallas kernels: 52.3 us -> 42.2 us  [on_device(): pl.pallas_call(functools.partial(kernel, nleaf, npair, n * nleaf * npair)...]
where the time goes in v3:
time: 45.2 us; the launch traced here: 45.1 us
  Pallas kernels  42.2 us (93%)
  local copies, waits for them, and re-layouts  2.24 us (5%)
  between operations  0.65 us (1%)
    pallas_call x1, Pallas kernels, on_device(): pl.pallas_call(functools.partial(kernel, nleaf, npair, n * nleaf * npair)...  42.2 us
    unnamed x4, local copies, waits for them, and re-layouts  2.24 us

profile of v3, /device:TPU:0, one launch (start us, length us, event | category | flops | bytes accessed | tf_op | source)
XLA Modules:
  0.0 45.1 jit_solution(13475238751073311881)
XLA Ops:
  0.6 42.2 %matern_step.1 = (f32[32,2048]{1,0:T(8,128)}, f32[2,32]{1,0:T(2,128)}) custom-call(f32[64,2048]{1,0:T(8,128)} %pts_ref.1, f32[1,64]{1,0:T(1,128)} %bitcast.1, f32[32,2048]{1,0:T(8,128)} %dir_ref.1, f32[32,2048]{1,0:T(8,128)} %res_ref.1, s32[1,32]{1,0:T(1,128)} %skel_ref.1), custom_call_target="tpu_custom_call" | custom-call | tf_op jit(solution)/shard_map/matern_step/pallas_call | solution.py:336
  42.8 0.0 copy-start
  42.8 1.7 %copy.9 = f32[32,2048]{1,0:T(8,128)} copy(f32[32,2048]{1,0:T(8,128)} %get-tuple-element.4) | data formatting | bytes 524288
  44.5 0.0 copy-done
  44.5 0.6 %copy.10 = f32[2,32]{1,0:T(2,128)} copy(f32[2,32]{1,0:T(2,128)S(1)} %copy-done) | data formatting | bytes 512
Async XLA Ops:
  42.8 1.7 %copy-start = (f32[2,32]{1,0:T(2,128)S(1)}, f32[2,32]{1,0:T(2,128)}, u32[]{:S(2)}) copy-start(f32[2,32]{1,0:T(2,128)} %get-tuple-element.5) | copy-start | bytes 772

commit v4 on v3

--- a/solution.py
+++ b/solution.py
@@ -219,7 +219,7 @@
 
     @pl.loop(0, n // CC)
     def _(ci):
-        @pl.when(ci == n // CC - 1)
+        @pl.when(ci == 1)
         def _():
             for k, c in enumerate(stage_a, 1):
                 src_rows = pl.ds(pl.multiple_of(lax.rem(leaf + nleaf - k, nleaf) * nskel, 8), nskel)

time: 45.2 us -> 44.4 us (0.982)
  Pallas kernels: 42.2 us -> 41.4 us
    pallas_call x1, Pallas kernels: 42.2 us -> 41.4 us  [on_device(): pl.pallas_call(functools.partial(kernel, nleaf, npair, n * nleaf * npair)...]
where the time goes in v4:
time: 44.4 us; the launch traced here: 44.3 us
  Pallas kernels  41.4 us (93%)
  local copies, waits for them, and re-layouts  2.24 us (5%)
  between operations  0.65 us (1%)
    pallas_call x1, Pallas kernels, on_device(): pl.pallas_call(functools.partial(kernel, nleaf, npair, n * nleaf * npair)...  41.4 us
    unnamed x4, local copies, waits for them, and re-layouts  2.24 us

profile of v4, /device:TPU:0, one launch (start us, length us, event | category | flops | bytes accessed | tf_op | source)
XLA Modules:
  0.0 44.3 jit_solution(10795026986556082491)
XLA Ops:
  0.6 41.4 %matern_step.1 = (f32[32,2048]{1,0:T(8,128)}, f32[2,32]{1,0:T(2,128)}) custom-call(f32[64,2048]{1,0:T(8,128)} %pts_ref.1, f32[1,64]{1,0:T(1,128)} %bitcast.1, f32[32,2048]{1,0:T(8,128)} %dir_ref.1, f32[32,2048]{1,0:T(8,128)} %res_ref.1, s32[1,32]{1,0:T(1,128)} %skel_ref.1), custom_call_target="tpu_custom_call" | custom-call | tf_op jit(solution)/shard_map/matern_step/pallas_call | solution.py:336
  42.0 0.0 copy-start
  42.0 1.7 %copy.9 = f32[32,2048]{1,0:T(8,128)} copy(f32[32,2048]{1,0:T(8,128)} %get-tuple-element.4) | data formatting | bytes 524288
  43.7 0.0 copy-done
  43.7 0.6 %copy.10 = f32[2,32]{1,0:T(2,128)} copy(f32[2,32]{1,0:T(2,128)S(1)} %copy-done) | data formatting | bytes 512
Async XLA Ops:
  42.0 1.7 %copy-start = (f32[2,32]{1,0:T(2,128)S(1)}, f32[2,32]{1,0:T(2,128)}, u32[]{:S(2)}) copy-start(f32[2,32]{1,0:T(2,128)} %get-tuple-element.5) | copy-start | bytes 772
